TPU v7x, 256 devices: a whole 4x4x8 slice. The times are simulated.
256 devices in a mesh: gx: 8 (over x, core), gy: 32 (over z, y).
Axes of the slice: x: 4, y: 4, z: 8, core: 2. Of those that a mesh axis runs over, the one named last changes fastest.
Arguments:
- volume: bfloat16 [64, 256, 2, 256], P('gx', 'gy'), may hold values from -6 to 6
- first_weight: bfloat16 [6912, 256], replicated, may hold values from -0.078125 to 0.078125
- second_weight: bfloat16 [6912, 256], replicated, may hold values from -0.078125 to 0.078125
- cotangent: bfloat16 [64, 256, 2, 256], P('gx', 'gy'), may hold values from -6 to 6
Outputs:
- output: bfloat16 [64, 256, 2, 256], P('gx', 'gy')
- volume_grad: bfloat16 [64, 256, 2, 256], P('gx', 'gy')
- second_grad: float32 [1769472], P(('gx', 'gy'))
All inputs are finite; a program needn't handle non-finite values.
Results may differ from a plain program's by a relative error of at most 0.015.
Values may be sent and summed in bfloat16 or wider, within the bound.
A program may use at most 64 MiB of HBM per device.

v0:
```python
import jax
import jax.numpy as jnp
from jax import lax
from jax.sharding import PartitionSpec as P


def padded_2(x, sides, width):
    for axis, dim in sides:
        devices, length = (lax.axis_size(axis), x.shape[dim])
        up = [(i, (i + 1) % devices) for i in range(devices)]
        down = [(j, i) for i, j in up]
        last = lax.slice_in_dim(x, length - width, length, axis=dim)
        first = lax.slice_in_dim(x, 0, width, axis=dim)
        before = lax.ppermute(last, axis, up)
        after = lax.ppermute(first, axis, down)
        x = jnp.concatenate([before, x, after], axis=dim)
    return x


def pad_faces(field):
    padded = padded_2(field, (("gx", 0), ("gy", 1)), 1)
    return padded


def correlate(padded, kernel):
    chans = padded.shape[3]
    weights = kernel.reshape(3, 3, 3, chans, kernel.shape[1])
    result = lax.conv_general_dilated(
        padded[None],
        weights,
        (1, 1, 1),
        [(0, 0), (0, 0), (1, 1)],
        dimension_numbers=("NDHWC", "DHWIO", "NDHWC"),
        preferred_element_type=jnp.float32,
    )
    return result[0]


def weight_term(padded, grad, scale):
    sx, sy, sz, chans = grad.shape
    full = jnp.pad(padded, ((0, 0), (0, 0), (1, 1), (0, 0)))
    columns = []
    for a in range(3):
        for b in range(3):
            for e in range(3):
                columns.append(full[a : a + sx, b : b + sy, e : e + sz, :])
    stacked = jnp.concatenate(columns, axis=-1).reshape(sx * sy * sz, 27 * padded.shape[3])
    product = lax.dot_general(
        stacked,
        grad.reshape(sx * sy * sz, chans),
        (((0,), (0,)), ((), ())),
        preferred_element_type=jnp.float32,
    )
    return (product * scale).reshape(-1)


def spread_sum(term):
    return lax.psum_scatter(term, ("gx", "gy"), scatter_dimension=0, tiled=True)


def turn_kernel(kernel):
    chans = kernel.shape[1]
    weights = kernel.reshape(3, 3, 3, chans, chans)[::-1, ::-1, ::-1]
    return jnp.transpose(weights, (0, 1, 2, 4, 3)).reshape(27 * chans, chans)


def body(volume, first_weight, second_weight, cotangent):
    sx, sy, sz, chans = volume.shape
    total = sx * lax.axis_size("gx") * sy * lax.axis_size("gy") * sz
    scale = 1.0 / jnp.sqrt(jnp.float32(total))
    vol_padded = pad_faces(volume)
    pre = correlate(vol_padded, first_weight)
    hidden = jax.nn.silu(pre).astype(jnp.bfloat16)
    hid_padded = pad_faces(hidden)
    output = correlate(hid_padded, second_weight).astype(jnp.bfloat16)
    cot_padded = pad_faces(cotangent)
    second_grad = spread_sum(weight_term(hid_padded, cotangent, scale))
    back = correlate(cot_padded, turn_kernel(second_weight))
    sig = jax.nn.sigmoid(pre)
    through = (back * sig * (1.0 + pre * (1.0 - sig))).astype(jnp.bfloat16)
    thr_padded = pad_faces(through)
    volume_grad = correlate(thr_padded, turn_kernel(first_weight)).astype(jnp.bfloat16)
    return (output, volume_grad, second_grad)


def solution(mesh):
    in_specs = (P("gx", "gy", None, None), P(), P(), P("gx", "gy", None, None))
    out_specs = (P("gx", "gy", None, None), P("gx", "gy", None, None), P(("gx", "gy")))
    return jax.shard_map(body, mesh=mesh, in_specs=in_specs, out_specs=out_specs, check_vma=False)
```

profile of v0, /device:TPU:1, one launch (start us, length us, event | category | flops | bytes accessed | tf_op | source)
XLA Modules:
  0.0 347.5 jit_solution(7034389863503954572)
XLA Ops:
  7.2 0.9 fusion.20
  8.1 2.6 collective-permute-start.8
  10.7 0.7 collective-permute-start.9
  11.4 0.7 fusion.22
  12.1 1.1 collective-permute-start
  13.2 1.9 collective-permute-start.1
  15.1 0.9 constant_dynamic-update-slice_fusion.4
  16.0 6.4 %collective-permute-start.11 = (bf16[10,1,2,256]{3,2,1,0:T(2,128)(2,1)S(1)}, bf16[10,1,2,256]{3,2,1,0:T(2,128)(2,1)S(1)}, u32[]{:S(2)}, u32[]{:S(2)}) collective-permute-start(bf16[10,1,2,256]{3,2,1,0:T(2,128)(2,1)S(1)} %get-tuple-element.16), channel_id=1, source_target_pairs={{1,0},{2,1},{3,2},{4,3},{5,4},{6,5},{7,6},{8,7},{9,8},{10,9},{11,1... | collective-permute-start | bytes 30728 | tf_op jit(solution)/shard_map/ppermute | solution.py:15
  22.4 0.9 constant_dynamic-update-slice_fusion.1
  23.4 4.9 %collective-permute-start.3 = (bf16[10,1,2,256]{3,2,1,0:T(2,128)(2,1)S(1)}, bf16[10,1,2,256]{3,2,1,0:T(2,128)(2,1)S(1)}, u32[]{:S(2)}, u32[]{:S(2)}) collective-permute-start(bf16[10,1,2,256]{3,2,1,0:T(2,128)(2,1)S(1)} %get-tuple-element.20), channel_id=1, source_target_pairs={{1,0},{2,1},{3,2},{4,3},{5,4},{6,5},{7,6},{8,7},{9,8},{10,9},{11,1... | collective-permute-start | bytes 30728 | tf_op jit(solution)/shard_map/ppermute | solution.py:15
  28.3 0.1 maximum_bitcast_fusion.1
  28.4 2.9 fusion.4
  31.3 2.7 collective-permute-done.2
  34.1 0.1 maximum_bitcast_fusion
  34.2 3.5 %fusion.7 = f32[1,8,8,2,256]{4,0,3,2,1:T(1,128)S(1)} fusion(bf16[3,3,3,256,256]{4,3,2,1,0:T(8,128)(2,1)S(1)} %bitcast.62, bf16[1,10,10,2,256]{4,3,2,1,0:T(2,128)(2,1)S(1)} %maximum_bitcast_fusion), kind=kOutput, calls=%fused_computation.28 | convolution fusion | flops 301989888 | bytes 3772416 | tf_op jit(solution)/shard_map/conv_general_dilated | solution.py:28
  37.8 0.9 fusion.10
  38.7 4.9 %collective-permute-start.5 = (bf16[1,8,2,256]{3,2,1,0:T(2,128)(2,1)S(1)}, bf16[1,8,2,256]{3,2,1,0:T(2,128)(2,1)S(1)}, u32[]{:S(2)}, u32[]{:S(2)}) collective-permute-start(bf16[1,8,2,256]{3,2,1,0:T(2,128)(2,1)S(1)} %get-tuple-element.26), channel_id=1, source_target_pairs={{32,0},{64,32},{96,64},{128,96},{160,128},{192,160},{224,192},{0,2... | collective-permute-start | bytes 24584 | tf_op jit(solution)/shard_map/ppermute | solution.py:15
  43.6 0.8 collective-permute-done.5
  44.4 0.3 collective-permute-done.4
  44.8 1.3 collective-permute-start.7
  46.1 0.3 collective-permute-start.6
  46.3 1.2 collective-permute-done.7
  47.5 4.4 %collective-permute-done.6 = bf16[10,1,2,256]{3,2,1,0:T(2,128)(2,1)S(1)} collective-permute-done((bf16[10,1,2,256]{3,2,1,0:T(2,128)(2,1)S(1)}, bf16[10,1,2,256]{3,2,1,0:T(2,128)(2,1)S(1)}, u32[]{:S(2)}, u32[]{:S(2)}) %collective-permute-start.6) | collective-permute-done | bytes 10272 | tf_op jit(solution)/shard_map/ppermute | solution.py:14
  51.9 0.2 pad_maximum_fusion
  52.2 0.2 pad_maximum_fusion.1
  52.4 0.1 constant_dynamic-update-slice_fusion.30
  52.9 0.1 constant_dynamic-update-slice_fusion.26
  53.1 0.1 constant_dynamic-update-slice_fusion.24
  53.2 0.1 constant_dynamic-update-slice_fusion.23
  53.4 0.1 constant_dynamic-update-slice_fusion.21
  54.8 0.1 constant_dynamic-update-slice_fusion.8
  55.0 0.1 constant_dynamic-update-slice_fusion.6
  55.1 4.1 %fusion.1 = f32[864,2,8,128]{3,2,1,0:T(8,128)} fusion(bf16[8,8,2,6912]{3,2,1,0:T(2,128)(2,1)S(1)} %constant_dynamic-update-slice_fusion.6, bf16[8,8,2,256]{3,2,1,0:T(2,128)(2,1)S(1)} %copy-done.3), kind=kOutput, calls=%fused_computation.2 | convolution fusion | flops 454754304 | bytes 8912896 | tf_op jit(solution)/shard_map/dot_general | solution.py:48
  59.2 9.5 %copy.34 = f32[864,2,8,128]{3,1,2,0:T(2,128)} copy(f32[864,2,8,128]{3,2,1,0:T(8,128)} %fusion.1) | data formatting | bytes 14155776
  68.7 1.3 fusion.19
  70.0 4.6 %collective-permute-start.13 = (bf16[1,8,2,256]{3,2,1,0:T(2,128)(2,1)}, bf16[1,8,2,256]{3,2,1,0:T(2,128)(2,1)}, u32[]{:S(2)}, u32[]{:S(2)}) collective-permute-start(bf16[1,8,2,256]{3,2,1,0:T(2,128)(2,1)} %get-tuple-element.22), channel_id=1, source_target_pairs={{32,0},{64,32},{96,64},{128,96},{160,128},{192,160},{224,192},{0,2... | collective-permute-start | bytes 24584 | tf_op jit(solution)/shard_map/ppermute | solution.py:15
  74.6 1.2 collective-permute-done.13
  75.8 0.3 collective-permute-done.12
  76.1 0.8 pad_maximum_fusion.6
  77.0 1.5 collective-permute-start.14
  78.5 1.0 fusion.27
  79.5 3.4 convolution_convert_fusion.1
  82.9 0.7 copy.29
  83.6 0.9 maximum_bitcast_fusion.2
  84.5 3.0 convolution_convert_fusion
  87.6 0.7 copy.30
  88.2 251.0 %all-reduce.4.cloned.1.call-done = f32[1769472]{0:T(1024)} async-done(((f32[1769472]{0:T(1024)}), f32[1769472]{0:T(1024)}) %all-reduce.4.cloned.1.call-update) | async-done | bytes 7077904
  339.2 1.4 dynamic-slice
  (62 shorter events, 2.3 us)
Async XLA Ops:
  7.2 21.3 %copy-start = (bf16[6912,256]{1,0:T(8,128)(2,1)S(1)}, bf16[6912,256]{1,0:T(8,128)(2,1)}, u32[]{:S(2)}) copy-start(bf16[6912,256]{1,0:T(8,128)(2,1)} %param.6) | copy-start | bytes 10616836
  7.2 332.0 %all-reduce.4.cloned.1.call-start = ((), (), s32[]{:S(2)}) async-start(), calls=%async_computation | async-start | bytes 14155776
  8.1 7.0 %collective-permute-start.8 = (bf16[1,8,2,256]{3,2,1,0:T(2,128)(2,1)S(1)}, bf16[1,8,2,256]{3,2,1,0:T(2,128)(2,1)S(1)}, u32[]{:S(2)}, u32[]{:S(2)}) collective-permute-start(bf16[1,8,2,256]{3,2,1,0:T(2,128)(2,1)S(1)} %get-tuple-element.24), channel_id=1, source_target_pairs={{0,32},{32,64},{64,96},{96,128},{128,160},{160,192},{192,224},{224... | collective-permute-start | bytes 24584 | tf_op jit(solution)/shard_map/ppermute | solution.py:14
  10.7 5.3 %collective-permute-start.9 = (bf16[1,8,2,256]{3,2,1,0:T(2,128)(2,1)S(1)}, bf16[1,8,2,256]{3,2,1,0:T(2,128)(2,1)S(1)}, u32[]{:S(2)}, u32[]{:S(2)}) collective-permute-start(bf16[1,8,2,256]{3,2,1,0:T(2,128)(2,1)S(1)} %get-tuple-element.23), channel_id=1, source_target_pairs={{32,0},{64,32},{96,64},{128,96},{160,128},{192,160},{224,192},{0,2... | collective-permute-start | bytes 24584 | tf_op jit(solution)/shard_map/ppermute | solution.py:15
  12.1 10.3 %collective-permute-start = (bf16[1,8,2,256]{3,2,1,0:T(2,128)(2,1)S(1)}, bf16[1,8,2,256]{3,2,1,0:T(2,128)(2,1)S(1)}, u32[]{:S(2)}, u32[]{:S(2)}) collective-permute-start(bf16[1,8,2,256]{3,2,1,0:T(2,128)(2,1)S(1)} %get-tuple-element.28), channel_id=1, source_target_pairs={{0,32},{32,64},{64,96},{96,128},{128,160},{160,192},{192,224},{224... | collective-permute-start | bytes 24584 | tf_op jit(solution)/shard_map/ppermute | solution.py:14
  13.2 10.1 %collective-permute-start.1 = (bf16[1,8,2,256]{3,2,1,0:T(2,128)(2,1)S(1)}, bf16[1,8,2,256]{3,2,1,0:T(2,128)(2,1)S(1)}, u32[]{:S(2)}, u32[]{:S(2)}) collective-permute-start(bf16[1,8,2,256]{3,2,1,0:T(2,128)(2,1)S(1)} %get-tuple-element.27), channel_id=1, source_target_pairs={{32,0},{64,32},{96,64},{128,96},{160,128},{192,160},{224,192},{0,2... | collective-permute-start | bytes 24584 | tf_op jit(solution)/shard_map/ppermute | solution.py:15
  16.0 12.2 %collective-permute-start.11 = (bf16[10,1,2,256]{3,2,1,0:T(2,128)(2,1)S(1)}, bf16[10,1,2,256]{3,2,1,0:T(2,128)(2,1)S(1)}, u32[]{:S(2)}, u32[]{:S(2)}) collective-permute-start(bf16[10,1,2,256]{3,2,1,0:T(2,128)(2,1)S(1)} %get-tuple-element.16), channel_id=1, source_target_pairs={{1,0},{2,1},{3,2},{4,3},{5,4},{6,5},{7,6},{8,7},{9,8},{10,9},{11,1... | collective-permute-start | bytes 30728 | tf_op jit(solution)/shard_map/ppermute | solution.py:15
  22.4 5.8 %collective-permute-start.10 = (bf16[10,1,2,256]{3,2,1,0:T(2,128)(2,1)S(1)}, bf16[10,1,2,256]{3,2,1,0:T(2,128)(2,1)S(1)}, u32[]{:S(2)}, u32[]{:S(2)}) collective-permute-start(bf16[10,1,2,256]{3,2,1,0:T(2,128)(2,1)S(1)} %get-tuple-element.15), channel_id=1, source_target_pairs={{0,1},{1,2},{2,3},{3,4},{4,5},{5,6},{6,7},{7,8},{8,9},{9,10},{10,1... | collective-permute-start | bytes 30728 | tf_op jit(solution)/shard_map/ppermute | solution.py:14
  23.4 8.0 %collective-permute-start.3 = (bf16[10,1,2,256]{3,2,1,0:T(2,128)(2,1)S(1)}, bf16[10,1,2,256]{3,2,1,0:T(2,128)(2,1)S(1)}, u32[]{:S(2)}, u32[]{:S(2)}) collective-permute-start(bf16[10,1,2,256]{3,2,1,0:T(2,128)(2,1)S(1)} %get-tuple-element.20), channel_id=1, source_target_pairs={{1,0},{2,1},{3,2},{4,3},{5,4},{6,5},{7,6},{8,7},{9,8},{10,9},{11,1... | collective-permute-start | bytes 30728 | tf_op jit(solution)/shard_map/ppermute | solution.py:15
  28.2 5.8 %collective-permute-start.2 = (bf16[10,1,2,256]{3,2,1,0:T(2,128)(2,1)S(1)}, bf16[10,1,2,256]{3,2,1,0:T(2,128)(2,1)S(1)}, u32[]{:S(2)}, u32[]{:S(2)}) collective-permute-start(bf16[10,1,2,256]{3,2,1,0:T(2,128)(2,1)S(1)} %get-tuple-element.19), channel_id=1, source_target_pairs={{0,1},{1,2},{2,3},{3,4},{4,5},{5,6},{6,7},{7,8},{8,9},{9,10},{10,1... | collective-permute-start | bytes 30728 | tf_op jit(solution)/shard_map/ppermute | solution.py:14
  28.4 5.8 %copy-start.6 = (bf16[6912,256]{1,0:T(8,128)(2,1)S(1)}, bf16[6912,256]{1,0:T(8,128)(2,1)}, u32[]{:S(2)}) copy-start(bf16[6912,256]{1,0:T(8,128)(2,1)} %param.5) | copy-start | bytes 10616836
  38.6 15.9 %copy-start.1 = (bf16[8,8,2,256]{3,2,1,0:T(2,128)(2,1)}, bf16[8,8,2,256]{3,2,1,0:T(2,128)(2,1)S(1)}, u32[]{:S(2)}) copy-start(bf16[8,8,2,256]{3,2,1,0:T(2,128)(2,1)S(1)} %get-tuple-element.10) | copy-start | bytes 196612
  38.7 5.8 %collective-permute-start.5 = (bf16[1,8,2,256]{3,2,1,0:T(2,128)(2,1)S(1)}, bf16[1,8,2,256]{3,2,1,0:T(2,128)(2,1)S(1)}, u32[]{:S(2)}, u32[]{:S(2)}) collective-permute-start(bf16[1,8,2,256]{3,2,1,0:T(2,128)(2,1)S(1)} %get-tuple-element.26), channel_id=1, source_target_pairs={{32,0},{64,32},{96,64},{128,96},{160,128},{192,160},{224,192},{0,2... | collective-permute-start | bytes 24584 | tf_op jit(solution)/shard_map/ppermute | solution.py:15
  43.6 1.2 collective-permute-start.4
  44.8 2.7 collective-permute-start.7
  46.1 5.8 %collective-permute-start.6 = (bf16[10,1,2,256]{3,2,1,0:T(2,128)(2,1)S(1)}, bf16[10,1,2,256]{3,2,1,0:T(2,128)(2,1)S(1)}, u32[]{:S(2)}, u32[]{:S(2)}) collective-permute-start(bf16[10,1,2,256]{3,2,1,0:T(2,128)(2,1)S(1)} %get-tuple-element.17), channel_id=1, source_target_pairs={{0,1},{1,2},{2,3},{3,4},{4,5},{5,6},{6,7},{7,8},{8,9},{9,10},{10,1... | collective-permute-start | bytes 30728 | tf_op jit(solution)/shard_map/ppermute | solution.py:14
  47.5 6.8 %copy-start.4 = (bf16[10,1,2,256]{3,2,1,0:T(2,128)(2,1)}, bf16[10,1,2,256]{3,2,1,0:T(2,128)(2,1)S(1)}, u32[]{:S(2)}) copy-start(bf16[10,1,2,256]{3,2,1,0:T(2,128)(2,1)S(1)} %collective-permute-done.7) | copy-start | bytes 30724
  51.9 2.4 copy-start.5
  52.7 2.4 copy-start.3
  70.0 5.7 %collective-permute-start.13 = (bf16[1,8,2,256]{3,2,1,0:T(2,128)(2,1)}, bf16[1,8,2,256]{3,2,1,0:T(2,128)(2,1)}, u32[]{:S(2)}, u32[]{:S(2)}) collective-permute-start(bf16[1,8,2,256]{3,2,1,0:T(2,128)(2,1)} %get-tuple-element.22), channel_id=1, source_target_pairs={{32,0},{64,32},{96,64},{128,96},{160,128},{192,160},{224,192},{0,2... | collective-permute-start | bytes 24584 | tf_op jit(solution)/shard_map/ppermute | solution.py:15
  74.6 1.5 collective-permute-start.12
  76.9 6.7 %collective-permute-start.15 = (bf16[10,1,2,256]{3,2,1,0:T(2,128)(2,1)S(1)}, bf16[10,1,2,256]{3,2,1,0:T(2,128)(2,1)S(1)}, u32[]{:S(2)}, u32[]{:S(2)}) collective-permute-start(bf16[10,1,2,256]{3,2,1,0:T(2,128)(2,1)S(1)} %get-tuple-element.14), channel_id=1, source_target_pairs={{1,0},{2,1},{3,2},{4,3},{5,4},{6,5},{7,6},{8,7},{9,8},{10,9},{11,1... | collective-permute-start | bytes 30728 | tf_op jit(solution)/shard_map/ppermute | solution.py:15
  77.0 6.6 %collective-permute-start.14 = (bf16[10,1,2,256]{3,2,1,0:T(2,128)(2,1)S(1)}, bf16[10,1,2,256]{3,2,1,0:T(2,128)(2,1)S(1)}, u32[]{:S(2)}, u32[]{:S(2)}) collective-permute-start(bf16[10,1,2,256]{3,2,1,0:T(2,128)(2,1)S(1)} %get-tuple-element.13), channel_id=1, source_target_pairs={{0,1},{1,2},{2,3},{3,4},{4,5},{5,6},{6,7},{7,8},{8,9},{9,10},{10,1... | collective-permute-start | bytes 30728 | tf_op jit(solution)/shard_map/ppermute | solution.py:14
  79.5 4.1 %copy-start.2 = (bf16[8,8,2,256]{3,2,1,0:T(2,128)(2,1)S(1)}, bf16[8,8,2,256]{3,2,1,0:T(2,128)(2,1)}, u32[]{:S(2)}) copy-start(bf16[8,8,2,256]{3,2,1,0:T(2,128)(2,1)} %get-tuple-element.9) | copy-start | bytes 196612
  79.5 5.0 %copy-start.7 = (bf16[6912,256]{1,0:T(8,128)(2,1)S(1)}, bf16[6912,256]{1,0:T(8,128)(2,1)}, u32[]{:S(2)}) copy-start(bf16[6912,256]{1,0:T(8,128)(2,1)} %param.5) | copy-start | bytes 10616836
Sparse Core Ops, SparseCore 0:
  68.8 270.3 all-reduce.3
where the time goes:
time: 349 us; the launch traced here: 347 us
  waiting for transfers between devices  262 us (75%)
  starting transfers between devices  30.1 us (9%)
  local copies, waits for them, and re-layouts  19.7 us (6%)
  matrix products  16.9 us (5%)
  between operations  14.4 us (4%)
  other arithmetic  4.42 us (1%)
    unnamed x2, waiting for transfers between devices  251 us
    ppermute x8, starting transfers between devices, padded_2(): after = lax.ppermute(first, axis, down)  24.6 us
    unnamed x48, local copies, waits for them, and re-layouts  16.6 us
    conv_general_dilated x4, matrix products, correlate(): lax.conv_general_dilated(padded[None], weights, (1, 1, 1), [(0, 0), (0, 0...  12.8 us
    ppermute x8, waiting for transfers between devices, padded_2(): before = lax.ppermute(last, axis, up)  7.84 us
  transfers between devices with their start and end apart: 17, of which 8 were waited for; matrix products, arithmetic and copies ran while one was open for 5% of the time, Pallas kernels for 0%

commit v1 on v0

v1 whole, which is shorter than its diff:
```python
import jax
import jax.numpy as jnp
import numpy as np
from jax import lax
from jax.experimental import pallas as pl
from jax.experimental.pallas import tpu as pltpu
from jax.sharding import PartitionSpec as P

C = 256
NGX = 8
NGY = 32
OWN = 64
ROWS = 27
PAD = 32
SLOTS = 5
F32 = jnp.float32
BF16 = jnp.bfloat16
MESH = pl.DeviceIdType.MESH


def strip_matrix():
    m = np.zeros((96, OWN), np.float32)
    for x in range(8):
        for j in range(2):
            m[x * 2 + j, x * 8 + 6 + j] = 1
            m[16 + x * 2 + j, x * 8 + j] = 1
    for i, (x0, y0) in enumerate(((6, 6), (6, 0), (0, 6), (0, 0))):
        for k in range(2):
            for j in range(2):
                m[32 + 16 * i + 2 * k + j, (x0 + k) * 8 + y0 + j] = 1
    return m


def window_matrices():
    own = np.zeros((192, OWN), np.float32)
    got = np.zeros((192, 128), np.float32)
    for xi in range(12):
        for yj in range(16):
            if 10 <= yj < 14:
                continue
            x, y, r = xi - 2, (yj if yj < 10 else yj - 16), xi * 16 + yj
            xs = -1 if x < 0 else (1 if x > 7 else 0)
            ys = -1 if y < 0 else (1 if y > 7 else 0)
            xr, yr = (x + 2 if xs < 0 else x - 8), (y + 2 if ys < 0 else y - 8)
            if xs == 0 and ys == 0:
                own[r, x * 8 + y] = 1
            elif ys == 0:
                got[r, (0 if xs < 0 else 16) + xr * 8 + y] = 1
            elif xs == 0:
                got[r, (32 if ys < 0 else 48) + x * 2 + yr] = 1
            else:
                base = 64 + (0 if xs < 0 else 32) + (0 if ys < 0 else 16)
                got[r, base + xr * 2 + yr] = 1
    return own, got


def dot(a, b):
    return jnp.dot(a, b, preferred_element_type=F32)


def dot_t(a, b):
    return lax.dot_general(a, b, (((1,), (1,)), ((), ())), preferred_element_type=F32)


def cyclic(x, shift):
    rows = x.shape[0]
    return pltpu.roll(x.reshape(rows // 16, 16, x.shape[1]), shift % 16, axis=1).reshape(rows, x.shape[1])


def corr(src, w, rows, z, flip):
    total = None
    for b in range(3):
        acc = None
        for a in range(3):
            if flip:
                tap = ((2 - a) * 3 + (2 - b)) * 3
                term = None
                for zi in range(2):
                    e = tap + 1 + z - zi
                    d = dot_t(src[16 * a : 16 * a + rows, zi * C : (zi + 1) * C], w[e * C : (e + 1) * C, :])
                    term = d if term is None else term + d
            else:
                tap = (a * 3 + b) * 3 + 1 - z
                term = dot(src[16 * a : 16 * a + rows, :], w[tap * C : (tap + 2) * C, :])
            acc = term if acc is None else acc + term
        if b != 1:
            acc = cyclic(acc, 1 - b)
        total = acc if total is None else total + acc
    return total


def own_rows(x, first):
    return x.reshape(x.shape[0] // 16, 16, C)[first : first + 8, 0:8, :].reshape(OWN, C)


def kernel(
    v_ref, c_ref, w1_hbm, w2_hbm, p_ref, qo_ref, qs_ref,
    out_ref, vg_ref, sg_ref,
    w1, w2, strips, got, ext, hext, text, pre, cg, cs, cgf, csf, hg, rbuf, grad, chunk, land,
    wsem, hsend, hrecv, csend, crecv, ssend, srecv, gsend, grecv, rsend, rrecv,
):
    gx, gy = lax.axis_index("gx"), lax.axis_index("gy")

    def at(dx, dy):
        return (lax.rem(gx + dx + NGX, NGX), lax.rem(gy + dy + NGY, NGY))

    barrier = pltpu.get_barrier_semaphore()
    near = [(1, 0), (-1, 0), (0, 1), (0, -1), (1, 1), (1, -1), (-1, 1), (-1, -1)]
    for dx, dy in near:
        pl.semaphore_signal(barrier, inc=1, device_id=at(dx, dy), device_id_type=MESH)
    for k in range(2, NGX - 1):
        pl.semaphore_signal(barrier, inc=1, device_id=at(k, 0), device_id_type=MESH)

    @pl.loop(2, NGY - 1)
    def _(k):
        pl.semaphore_signal(barrier, inc=1, device_id=at(0, k), device_id_type=MESH)

    copies_w = [
        pltpu.make_async_copy(w1_hbm, w1, wsem.at[0]),
        pltpu.make_async_copy(w2_hbm, w2, wsem.at[1]),
    ]
    for c in copies_w:
        c.start()
    for i, ref in enumerate((v_ref, c_ref)):
        strips[i] = dot(p_ref[...], ref[...]).astype(BF16)
    pl.semaphore_wait(barrier, len(near) + (NGX - 3) + (NGY - 3))

    halo = []
    for i, ref in enumerate((v_ref, c_ref)):
        sources = [ref.at[48:64], ref.at[0:16]] + [strips.at[i, 16 * n : 16 * n + 16] for n in range(6)]
        row = []
        for n, (dx, dy) in enumerate(near):
            row.append(pltpu.make_async_remote_copy(
                src_ref=sources[n], dst_ref=got.at[i, 16 * n : 16 * n + 16],
                send_sem=hsend.at[i, n], recv_sem=hrecv.at[i, n],
                device_id=at(dx, dy), device_id_type=MESH))
            row[-1].start()
        halo.append(row)

    def to_ring(src, dst, send, recv):
        out = []
        for k in range(1, NGX):
            out.append(pltpu.make_async_remote_copy(
                src_ref=src, dst_ref=dst.at[gx], send_sem=send.at[k], recv_sem=recv.at[k],
                device_id=at(k, 0), device_id_type=MESH))
            out[-1].start()
        return out

    craw = to_ring(c_ref, cg, csend, crecv)
    cg[gx] = c_ref[...]

    for n in range(8):
        halo[0][n].wait_recv()
    ext[0] = (dot(qo_ref[...], v_ref[...]) + dot(qs_ref[...], got[0])).astype(BF16)
    for n in range(8):
        halo[1][n].wait_recv()
    cstrip = to_ring(got.at[1, 32:64], cs, ssend, srecv)
    cs[gx] = got[1, 32:64, :]
    ext[1] = (dot(qo_ref[...], c_ref[...]) + dot(qs_ref[...], got[1])).astype(BF16)

    copies_w[0].wait()
    tall = []
    for z in range(2):
        p = corr(ext.at[0], w1, 160, z, False)
        pre[:, z * C : (z + 1) * C] = p
        h = p / (1.0 + jnp.exp(-p))
        hext[:, z * C : (z + 1) * C] = h.astype(BF16)
        tall.append(own_rows(h, 1))
    hg[gx] = jnp.transpose(jnp.concatenate(tall, axis=0)).astype(BF16)
    hid = to_ring(hg.at[gx], hg, gsend, grecv)

    for c in craw + cstrip:
        c.wait_recv()
    for g in range(NGX):
        for z in range(2):
            cgf[z, 64 * g : 64 * g + 64, :] = cg[g, :, z * C : (z + 1) * C].astype(F32)
            csf[z, 32 * g : 32 * g + 32, :] = cs[g, :, z * C : (z + 1) * C].astype(F32)

    first = (gx * ROWS * NGY) // C
    offset = gx * ROWS * NGY - first * C
    lane8 = lax.broadcasted_iota(jnp.int32, (8, C), 0)

    @pl.loop(0, SLOTS * NGX)
    def _(it):
        s = it // NGX
        g = it - s * NGX
        t = jnp.minimum(first + s, 26)
        a = t // 9
        b = (t // 3) - 3 * a
        e = t - 9 * a - 3 * b
        edge = jnp.where(b == 0, 7, jnp.where(b == 2, 0, 8))
        turn = jnp.where(b == 0, 7, jnp.where(b == 2, 1, 0))
        side = jnp.where(b == 0, 16, 1)
        for z in range(2):
            zs = jnp.where(e == 0, 1, 0) if z == 0 else jnp.where(e == 2, 0, 1)
            keep = (e < 2) if z == 0 else (e > 0)
            for pair in range(4):
                blocks = []
                for xl in (2 * pair, 2 * pair + 1):
                    xs = lax.rem(g * 8 + xl + 1 - a + 64, 64)
                    gs = xs // 8
                    block = cgf[zs, pl.ds(pl.multiple_of(xs * 8, 8), 8), :]
                    line = csf[zs, pl.ds(gs * 32 + side + 2 * (xs - gs * 8), 1), :]
                    block = pltpu.roll(block, turn, axis=0)
                    block = jnp.where(lane8 == edge, line, block)
                    blocks.append(jnp.where(keep, block, 0.0))
                rbuf[s, pl.ds(pl.multiple_of(g * 128 + z * 64 + pair * 16, 16), 16), :] = (
                    jnp.concatenate(blocks, axis=0).astype(BF16))

    copies_w[1].wait()
    for z in range(2):
        o = corr(hext, w2, 128, z, False)
        out_ref[:, z * C : (z + 1) * C] = own_rows(o, 0).astype(BF16)

    for c in hid:
        c.wait_recv()

    @pl.loop(0, SLOTS)
    def _(s):
        acc = None
        for j in range(4):
            left = jnp.concatenate([hg[2 * j], hg[2 * j + 1]], axis=1)
            term = dot(left, rbuf[s, j * C : (j + 1) * C, :])
            acc = term if acc is None else acc + term
        for h in range(2):
            grad[h, pl.ds(pl.multiple_of(s * C, C), C), :] = acc[:, 128 * h : 128 * h + 128]

    def rows_of(j):
        return jnp.concatenate([grad[h, pl.ds(offset + ROWS * j, PAD), :] for h in range(2)], axis=1)

    def share(d):
        return pltpu.make_async_remote_copy(
            src_ref=chunk.at[d], dst_ref=land.at[d], send_sem=rsend.at[d], recv_sem=rrecv.at[d],
            device_id=at(0, d), device_id_type=MESH)

    @pl.loop(1, NGY)
    def _(d):
        j = lax.rem(gy + d, NGY)
        chunk[d] = rows_of(j).astype(BF16)
        share(d).start()

    for z in range(2):
        bk = corr(ext.at[1], w2, 160, z, True)
        p = pre[:, z * C : (z + 1) * C]
        sg = 1.0 / (1.0 + jnp.exp(-p))
        text[:, z * C : (z + 1) * C] = (bk * sg * (1.0 + p * (1.0 - sg))).astype(BF16)
    for z in range(2):
        o = corr(text, w1, 128, z, True)
        vg_ref[:, z * C : (z + 1) * C] = own_rows(o, 0).astype(BF16)

    sg_ref[...] = rows_of(gy)

    @pl.loop(1, NGY)
    def _(d):
        share(d).wait_recv()
        sg_ref[...] += land[d].astype(F32)

    sg_ref[...] = sg_ref[...] * np.float32(1.0 / np.sqrt(np.float32(32768.0)))

    @pl.loop(1, NGY)
    def _(d):
        share(d).wait_send()

    for c in halo[0] + halo[1] + craw + cstrip + hid:
        c.wait_send()


def body(volume, first_weight, second_weight, cotangent):
    vmem = pl.BlockSpec(memory_space=pltpu.VMEM)
    hbm = pl.BlockSpec(memory_space=pl.ANY)
    own, got = window_matrices()
    dma = pltpu.SemaphoreType.DMA
    scratch = [
        pltpu.VMEM((27 * C, C), BF16),
        pltpu.VMEM((27 * C, C), BF16),
        pltpu.VMEM((2, 96, 2 * C), BF16),
        pltpu.VMEM((2, 128, 2 * C), BF16),
        pltpu.VMEM((2, 192, 2 * C), BF16),
        pltpu.VMEM((160, 2 * C), BF16),
        pltpu.VMEM((160, 2 * C), BF16),
        pltpu.VMEM((160, 2 * C), F32),
        pltpu.VMEM((NGX, OWN, 2 * C), BF16),
        pltpu.VMEM((NGX, 32, 2 * C), BF16),
        pltpu.VMEM((2, 512, C), F32),
        pltpu.VMEM((2, 256, C), F32),
        pltpu.VMEM((NGX, C, 128), BF16),
        pltpu.VMEM((SLOTS, 1024, C), BF16),
        pltpu.VMEM((2, SLOTS * C, 128), F32),
        pltpu.VMEM((NGY, PAD, C), BF16),
        pltpu.VMEM((NGY, PAD, C), BF16),
        dma((2,)), dma((2, 8)), dma((2, 8)),
        dma((NGX,)), dma((NGX,)), dma((NGX,)), dma((NGX,)), dma((NGX,)), dma((NGX,)),
        dma((NGY,)), dma((NGY,)),
    ]
    out, vg, sg = pl.pallas_call(
        kernel,
        out_shape=(
            jax.ShapeDtypeStruct((OWN, 2 * C), BF16),
            jax.ShapeDtypeStruct((OWN, 2 * C), BF16),
            jax.ShapeDtypeStruct((PAD, C), F32),
        ),
        in_specs=[vmem, vmem, hbm, hbm, vmem, vmem, vmem],
        out_specs=(vmem, vmem, vmem),
        scratch_shapes=scratch,
        compiler_params=pltpu.CompilerParams(
            collective_id=0, has_side_effects=True, vmem_limit_bytes=48 * 2**20),
    )(
        volume.reshape(OWN, 2 * C), cotangent.reshape(OWN, 2 * C), first_weight, second_weight,
        jnp.asarray(strip_matrix(), BF16), jnp.asarray(own, BF16), jnp.asarray(got, BF16),
    )
    return out.reshape(volume.shape), vg.reshape(volume.shape), sg[:ROWS].reshape(-1)


def solution(mesh):
    in_specs = (P("gx", "gy", None, None), P(), P(), P("gx", "gy", None, None))
    out_specs = (P("gx", "gy", None, None), P("gx", "gy", None, None), P(("gx", "gy")))
    return jax.shard_map(body, mesh=mesh, in_specs=in_specs, out_specs=out_specs, check_vma=False)
```

time: 349 us -> 57.5 us (0.16)
  the two profiles are of different devices: /device:TPU:1 before, /device:TPU:6 now
where the time goes in v1:
time: 57.5 us; the launch traced here: 57.1 us
  Pallas kernels  48.5 us (84%)
  local copies, waits for them, and re-layouts  8 us (14%)
  between operations  0.66 us (1%)
    pallas_call x1, Pallas kernels, body(): pl.pallas_call(kernel, out_shape=(jax.ShapeDtypeStruct((OWN, 2 * C), BF16...  48.5 us
    unnamed x12, local copies, waits for them, and re-layouts  7.39 us

profile of v1, /device:TPU:6, one launch (start us, length us, event | category | flops | bytes accessed | tf_op | source)
XLA Modules:
  0.0 57.1 jit_solution(6908836461129021158)
XLA Ops:
  0.6 0.8 %copy.12 = bf16[8,8,2,256]{3,1,2,0:T(8,128)(2,1)S(1)} copy(bf16[8,8,2,256]{3,2,1,0:T(2,128)(2,1)} %param.7) | data formatting | bytes 131072
  1.5 0.9 %copy.13 = bf16[8,8,2,256]{3,1,2,0:T(8,128)(2,1)S(1)} copy(bf16[8,8,2,256]{3,2,1,0:T(2,128)(2,1)} %param.10) | data formatting | bytes 131072
  2.3 0.0 copy-start
  2.3 2.0 %copy-done = bf16[6912,256]{1,0:T(8,128)(2,1)S(1)} copy-done((bf16[6912,256]{1,0:T(8,128)(2,1)S(1)}, bf16[6912,256]{1,0:T(8,128)(2,1)}, u32[]{:S(2)}) %copy-start) | copy-done | bytes 3538968
  4.3 0.0 copy-start.1
  4.3 0.8 %copy-done.1 = bf16[192,128]{1,0:T(8,128)(2,1)S(1)} copy-done((bf16[192,128]{1,0:T(8,128)(2,1)S(1)}, bf16[192,128]{1,0:T(8,128)(2,1)}, u32[]{:S(2)}) %copy-start.1) | copy-done | bytes 49176
  5.1 0.0 copy-start.2
  5.1 0.8 %copy-done.2 = bf16[192,64]{1,0:T(8,128)(2,1)S(1)} copy-done((bf16[192,64]{1,0:T(8,128)(2,1)S(1)}, bf16[192,64]{1,0:T(8,128)(2,1)}, u32[]{:S(2)}) %copy-start.2) | copy-done | bytes 24600
  5.9 0.0 copy-start.3
  5.9 0.7 %copy-done.3 = bf16[96,64]{1,0:T(8,128)(2,1)S(1)} copy-done((bf16[96,64]{1,0:T(8,128)(2,1)S(1)}, bf16[96,64]{1,0:T(8,128)(2,1)}, u32[]{:S(2)}) %copy-start.3) | copy-done | bytes 12312
  6.7 48.5 %shard_map.94 = (bf16[64,512]{1,0:T(8,128)(2,1)S(1)}, bf16[64,512]{1,0:T(8,128)(2,1)S(1)}, f32[32,256]{1,0:T(8,128)S(1)}) custom-call(bf16[64,512]{1,0:T(8,128)(2,1)S(1)} %bitcast.9, bf16[64,512]{1,0:T(8,128)(2,1)S(1)} %bitcast.10, bf16[6912,256]{1,0:T(8,128)(2,1)S(1)} %copy-done, bf16[6912,256]{1,0:T(8,128)(2,1)} %w2_hbm.1, bf16[96,64]{1,0:T(8,128)(2,1)S(1)} %copy-done.3, ...), custom_call_target="tpu_custom_call" | custom-call | tf_op jit(solution)/shard_map/pallas_call | solution.py:295
  55.2 0.7 %copy.10 = bf16[8,8,2,256]{3,2,1,0:T(2,128)(2,1)} copy(bf16[8,8,2,256]{3,1,2,0:T(8,128)(2,1)S(1)} %bitcast.12) | data formatting | bytes 131072
  55.8 0.7 %copy.11 = bf16[8,8,2,256]{3,2,1,0:T(2,128)(2,1)} copy(bf16[8,8,2,256]{3,1,2,0:T(8,128)(2,1)S(1)} %bitcast.11) | data formatting | bytes 131072
  56.5 0.6 %reshape.25 = f32[6912]{0:T(1024)} reshape(f32[27,256]{1,0:T(8,128)S(1)} %bitcast.13) | data formatting | bytes 55296 | tf_op jit(solution)/shard_map/reshape | solution.py:311
Async XLA Ops:
  2.3 2.0 %copy-start = (bf16[6912,256]{1,0:T(8,128)(2,1)S(1)}, bf16[6912,256]{1,0:T(8,128)(2,1)}, u32[]{:S(2)}) copy-start(bf16[6912,256]{1,0:T(8,128)(2,1)} %w1_hbm.1) | copy-start | bytes 10616836
  4.3 0.8 %copy-start.1 = (bf16[192,128]{1,0:T(8,128)(2,1)S(1)}, bf16[192,128]{1,0:T(8,128)(2,1)}, u32[]{:S(2)}) copy-start(bf16[192,128]{1,0:T(8,128)(2,1)} %constant.8.clone.qs_ref) | copy-start | bytes 147460
  5.1 0.8 %copy-start.2 = (bf16[192,64]{1,0:T(8,128)(2,1)S(1)}, bf16[192,64]{1,0:T(8,128)(2,1)}, u32[]{:S(2)}) copy-start(bf16[192,64]{1,0:T(8,128)(2,1)} %constant.7.clone.qo_ref) | copy-start | bytes 73732
  5.9 0.7 %copy-start.3 = (bf16[96,64]{1,0:T(8,128)(2,1)S(1)}, bf16[96,64]{1,0:T(8,128)(2,1)}, u32[]{:S(2)}) copy-start(bf16[96,64]{1,0:T(8,128)(2,1)} %constant.6.clone.p_ref) | copy-start | bytes 36868
